TPU v7x, 32 devices: a whole 2x2x4 slice. The times are simulated.
32 devices in a mesh: pair: 8 (over z, x), occ: 4 (over y, core).
Axes of the slice: x: 2, y: 2, z: 4, core: 2. Of those that a mesh axis runs over, the one named last changes fastest.
Arguments:
- integrals: bfloat16 [8, 64, 64, 1024], P('pair', None, None, 'occ'), may hold values from -6 to 6
- occ_coeffs: bfloat16 [6144, 128], replicated, may hold values from -0.125 to 0.125
- virt_coeffs: bfloat16 [6144, 5120], P(None, 'pair'), may hold values from -0.078125 to 0.078125
- block_ids: int32 [2, 8, 64], P(None, 'pair'), may hold values from 0 to 95, as said below
- live_mask: int32 [8, 64], P('pair'), may hold values from 0 to 1, as said below
Outputs:
- factors: bfloat16 [128, 16, 5120], P('occ', None, 'pair')
Inputs may be any that keep to these rules, and one draw needn't show every extreme that they name: `block_ids`: slot s of pair index p holds a nu block N with N // 12 == s // 8; each (mu block, nu block) pair is held by at most one slot of all pair indices. `live_mask`: among the 8 slots s with the same s // 8 of one pair index, at most 4 are 1, and exactly 4 for some such group of every pair index.
All inputs are finite; a program needn't handle non-finite values.
Results may differ from a plain program's by a relative error of at most 0.017.
Values may be sent and summed in bfloat16 or wider, within the bound.
No kernel may reach another device: no remote copies, remote signals or barrier semaphores. Data moves between devices by JAX's collectives and lax.ppermute only.
A program may use at most 64 MiB of HBM per device.

v0:
```python
import jax
import jax.numpy as jnp
from jax import lax
from jax.sharding import PartitionSpec as P

LIVE = 4


def half_transform(block_data, mu_index, coeff_blocks):
    slot_count, block_width = (block_data.shape[0], block_data.shape[1])
    aux_local = block_data.shape[2] // block_width
    coeff_rows = jnp.take(coeff_blocks, mu_index, axis=0)
    shaped = block_data.reshape(slot_count, block_width, aux_local, block_width)
    return jnp.einsum("snqm,smi->snqi", shaped, coeff_rows, preferred_element_type=jnp.float32)


def on_device(integrals, occ_coeffs, virt_coeffs, block_ids, live_mask):
    blocks = integrals[0]
    slot_count, block_width = (blocks.shape[0], blocks.shape[1])
    aux_local = blocks.shape[2] // block_width
    occ_count = occ_coeffs.shape[1]
    block_count = occ_coeffs.shape[0] // block_width
    owners = lax.axis_size("pair")
    owned_count = block_count // owners
    group_size = slot_count // owners
    coeff_blocks = occ_coeffs.reshape(block_count, block_width, occ_count)
    mu_index = block_ids[0, 0]
    nu_index = block_ids[1, 0]
    live_flags = live_mask[0]
    grouped_live = live_flags.reshape(owners, group_size)
    sort_keys = (1 - grouped_live) * group_size + jnp.arange(group_size)[None, :]
    chosen = jnp.argsort(sort_keys, axis=1)[:, :LIVE]
    valid_flags = jnp.take_along_axis(grouped_live, chosen, axis=1).reshape(-1)
    slot_index = (chosen + jnp.arange(owners)[:, None] * group_size).reshape(-1)
    send_blocks = blocks[slot_index] * valid_flags[:, None, None].astype(jnp.bfloat16)
    send_blocks = send_blocks.reshape(owners, LIVE, block_width, aux_local * block_width)
    send_mu = mu_index[slot_index].reshape(owners, LIVE)
    send_nu = nu_index[slot_index].reshape(owners, LIVE)
    got_blocks, got_mu, got_nu = (
        lax.all_to_all(send_blocks, "pair", split_axis=0, concat_axis=0, tiled=True),
        lax.all_to_all(send_mu, "pair", split_axis=0, concat_axis=0, tiled=True),
        lax.all_to_all(send_nu, "pair", split_axis=0, concat_axis=0, tiled=True),
    )
    partial_terms = half_transform(
        got_blocks.reshape(owners * LIVE, block_width, -1), got_mu.reshape(-1), coeff_blocks
    )
    selector = got_nu.reshape(-1)[None, :] % owned_count == jnp.arange(owned_count)[:, None]
    summed = jnp.dot(
        selector.astype(jnp.float32),
        partial_terms.reshape(owners * LIVE, -1),
        precision=lax.Precision.HIGHEST,
    )
    summed = summed.reshape(owned_count, block_width, aux_local, occ_count)
    half_sums = summed.astype(jnp.bfloat16)
    slab_sums = lax.all_to_all(half_sums, "occ", split_axis=3, concat_axis=2, tiled=True)
    aux_count, slab_rows = (slab_sums.shape[2], slab_sums.shape[3])
    shard_piece = lax.all_gather(slab_sums, "pair", axis=0, tiled=True)
    piece_blocks = shard_piece.shape[0]
    flat_piece = shard_piece.reshape(piece_blocks * block_width, aux_count, slab_rows)
    result = jnp.einsum("nqi,na->iqa", flat_piece, virt_coeffs, preferred_element_type=jnp.float32)
    return result.astype(jnp.bfloat16)


def solution(mesh):
    return jax.shard_map(
        on_device,
        mesh=mesh,
        in_specs=(
            P("pair", None, None, "occ"),
            P(),
            P(None, "pair"),
            P(None, "pair", None),
            P("pair", None),
        ),
        out_specs=P("occ", None, "pair"),
        check_vma=False,
    )
```

profile of v0, /device:TPU:0, one launch (start us, length us, event | category | flops | bytes accessed | tf_op | source)
XLA Modules:
  0.0 337.0 jit_solution(16466119769843120083)
XLA Ops:
  6.5 0.8 slice_bitcast_fusion.1
  7.9 1.2 reduce.12
  9.3 0.7 sort.17
  10.1 0.7 gather_fusion.4
  11.1 0.7 gather_fusion.2
  11.8 0.7 all_to_all.31
  12.5 7.3 %all-to-all-start.2 = ((s32[8,1,4]{2,1,0:T(1,128)}), s32[8,1,4]{2,1,0:T(1,128)S(1)}, u32[]{:S(2)}, u32[]{:S(2)}) async-start(s32[8,1,4]{2,1,0:T(1,128)} %bitcast.9), calls=%async_computation.2 | async-start | bytes 8192 | tf_op jit(solution)/shard_map/all_to_all | solution.py:41
  19.9 0.7 gather_fusion
  20.6 0.7 all_to_all.28
  21.9 4.3 %all-to-all-done.2 = s32[8,1,4]{2,1,0:T(1,128)S(1)} async-done(((s32[8,1,4]{2,1,0:T(1,128)}), s32[8,1,4]{2,1,0:T(1,128)S(1)}, u32[]{:S(2)}, u32[]{:S(2)}) %all-to-all-start.2) | async-done | bytes 160 | tf_op jit(solution)/shard_map/all_to_all | solution.py:41
  26.2 3.3 all-to-all-start
  29.6 1.1 broadcast_multiply_fusion
  30.7 5.3 %all-to-all-done = s32[8,1,4]{2,1,0:T(1,128)S(1)} async-done(((s32[8,1,4]{2,1,0:T(1,128)}), s32[8,1,4]{2,1,0:T(1,128)S(1)}, u32[]{:S(2)}, u32[]{:S(2)}) %all-to-all-start) | async-done | bytes 160 | tf_op jit(solution)/shard_map/all_to_all | solution.py:42
  36.0 3.6 %all-to-all-start.1 = ((bf16[8,4,64,256]{3,2,1,0:T(8,128)(2,1)}), bf16[8,4,64,256]{3,2,1,0:T(8,128)(2,1)S(1)}, u32[]{:S(2)}, u32[]{:S(2)}) async-start(bf16[8,4,64,256]{3,2,1,0:T(8,128)(2,1)} %broadcast_multiply_fusion), calls=%async_computation.1 | async-start | bytes 2097152 | tf_op jit(solution)/shard_map/all_to_all | solution.py:40
  40.5 2.8 gather_fusion.3
  43.3 19.8 %all-to-all-done.1 = bf16[8,4,64,256]{3,2,1,0:T(8,128)(2,1)S(1)} async-done(((bf16[8,4,64,256]{3,2,1,0:T(8,128)(2,1)}), bf16[8,4,64,256]{3,2,1,0:T(8,128)(2,1)S(1)}, u32[]{:S(2)}, u32[]{:S(2)}) %all-to-all-start.1) | async-done | bytes 1048608 | tf_op jit(solution)/shard_map/all_to_all | solution.py:40
  63.1 0.8 reshape_reshape.3
  64.0 1.8 fusion.4
  65.8 5.6 %copy.44 = f32[32,64,4,128]{3,2,1,0:T(4,128)} copy(f32[32,64,4,128]{3,1,2,0:T(8,128)S(1)} %fusion.4) | data formatting | bytes 8388608 | tf_op jit(solution)/shard_map/snqm,smi->snqi/dot_general | solution.py:14
  71.3 5.7 %reshape.146 = f32[32,32768]{1,0:T(8,128)} reshape(f32[32,64,4,128]{3,2,1,0:T(4,128)} %copy.44) | data formatting | bytes 8388608 | tf_op jit(solution)/shard_map/reshape | solution.py:50
  77.0 6.0 %dot_general.15 = f32[64,4,128,32]{2,1,0,3:T(4,128)} reshape(f32[32768,32]{0,1:T(8,128)} %bitcast.54) | data formatting | bytes 8388608 | tf_op jit(solution)/shard_map/dot_general | solution.py:48
  83.0 5.9 %fusion.6 = bf16[12,64,4,128]{3,0,2,1:T(8,128)(2,1)S(1)} fusion(f32[64,4,128,32]{2,1,0,3:T(4,128)} %dot_general.15, s32[32]{0:T(128)S(1)} %and_select_fusion), kind=kOutput, calls=%fused_computation.11 | convolution fusion | flops 151388544 | bytes 4980864 | tf_op jit(solution)/shard_map/dot_general | solution.py:48
  88.9 4.1 %copy.46 = bf16[12,64,4,128]{1,2,0,3:T(4,128)(2,1)S(1)} copy(bf16[12,64,4,128]{3,0,2,1:T(8,128)(2,1)S(1)} %fusion.6) | data formatting | bytes 1572864 | tf_op jit(solution)/shard_map/convert_element_type | solution.py:54
  93.0 1.4 reshape.218
  94.4 14.7 %all_to_all.41 = bf16[4,2,49152]{2,1,0:T(2,128)(2,1)} all-to-all(bf16[4,2,49152]{2,1,0:T(2,128)(2,1)S(1)} %reshape.218), channel_id=1, replica_groups=mesh['pair'=8,'occ'=4] {'occ'}, dimensions={0} | all-to-all | bytes 1572864 | tf_op jit(solution)/shard_map/all_to_all | solution.py:55
  109.1 2.8 reshape.219
  112.3 1.6 copy.48
  113.9 174.2 %all-gather.2.cloned.1.call-done = bf16[96,64,16,32]{1,3,2,0:T(8,128)(2,1)} async-done(((bf16[12,64,16,32]{1,3,2,0:T(8,128)(2,1)}), bf16[96,64,16,32]{1,3,2,0:T(8,128)(2,1)}) %all-gather.2.cloned.1.call-update) | async-done | bytes 6291472 | tf_op jit(solution)/shard_map/all_gather | solution.py:57
  288.1 14.5 %copy.49 = bf16[96,64,16,32]{1,0,3,2:T(8,128)(2,1)} copy(bf16[96,64,16,32]{1,3,2,0:T(8,128)(2,1)} %all-gather.2.cloned.1.call-done) | data formatting | bytes 12582912 | tf_op jit(solution)/shard_map/all_gather | solution.py:57
  302.6 16.9 %reshape.147 = bf16[6144,16,32]{0,2,1:T(8,128)(2,1)} reshape(bf16[96,64,16,32]{1,0,3,2:T(8,128)(2,1)} %copy.49) | data formatting | bytes 12582912 | tf_op jit(solution)/shard_map/reshape | solution.py:59
  319.5 9.6 %fusion.12 = bf16[32,16,640]{2,0,1:T(8,128)(2,1)S(1)} fusion(bf16[6144,16,32]{0,2,1:T(8,128)(2,1)} %reshape.147, bf16[6144,640]{1,0:T(8,128)(2,1)} %param.7), kind=kOutput, calls=%fused_computation.13 | convolution fusion | flops 4026859520 | bytes 14811136 | tf_op jit(solution)/shard_map/nqi,na->iqa/dot_general | solution.py:60
  329.1 1.0 copy.50
  (34 shorter events, 3.2 us)
Async XLA Ops:
  6.5 14.7 %copy-start = (bf16[1,64,64,256]{3,2,1,0:T(8,128)(2,1)S(1)}, bf16[1,64,64,256]{3,2,1,0:T(8,128)(2,1)}, u32[]{:S(2)}) copy-start(bf16[1,64,64,256]{3,2,1,0:T(8,128)(2,1)} %param.5) | copy-start | bytes 6291460
  12.5 13.7 %all-to-all-start.2 = ((s32[8,1,4]{2,1,0:T(1,128)}), s32[8,1,4]{2,1,0:T(1,128)S(1)}, u32[]{:S(2)}, u32[]{:S(2)}) async-start(s32[8,1,4]{2,1,0:T(1,128)} %bitcast.9), calls=%async_computation.2 | async-start | bytes 8192 | tf_op jit(solution)/shard_map/all_to_all | solution.py:41
  26.2 9.8 %all-to-all-start = ((s32[8,1,4]{2,1,0:T(1,128)}), s32[8,1,4]{2,1,0:T(1,128)S(1)}, u32[]{:S(2)}, u32[]{:S(2)}) async-start(s32[8,1,4]{2,1,0:T(1,128)} %bitcast.2), calls=%async_computation | async-start | bytes 8192 | tf_op jit(solution)/shard_map/all_to_all | solution.py:42
  36.0 27.1 %all-to-all-start.1 = ((bf16[8,4,64,256]{3,2,1,0:T(8,128)(2,1)}), bf16[8,4,64,256]{3,2,1,0:T(8,128)(2,1)S(1)}, u32[]{:S(2)}, u32[]{:S(2)}) async-start(bf16[8,4,64,256]{3,2,1,0:T(8,128)(2,1)} %broadcast_multiply_fusion), calls=%async_computation.1 | async-start | bytes 2097152 | tf_op jit(solution)/shard_map/all_to_all | solution.py:40
  39.6 248.5 %all-gather.2.cloned.1.call-start = ((), (), s32[]{:S(2)}) async-start(), calls=%async_computation.4 | async-start | bytes 14155776 | tf_op jit(solution)/shard_map/all_gather | solution.py:57
  319.5 10.6 %copy-start.1 = (bf16[1,64,64,256]{3,2,1,0:T(8,128)(2,1)S(1)}, bf16[1,64,64,256]{3,2,1,0:T(8,128)(2,1)}, u32[]{:S(2)}) copy-start(bf16[1,64,64,256]{3,2,1,0:T(8,128)(2,1)} %param.5) | copy-start | bytes 6291460
Sparse Core Ops, SparseCore 0:
  114.1 173.9 all-gather.1
where the time goes:
time: 338 us; the launch traced here: 337 us
  waiting for transfers between devices  204 us (60%)
  local copies, waits for them, and re-layouts  70 us (21%)
  matrix products  17.3 us (5%)
  blocking collectives  14.7 us (4%)
  starting transfers between devices  14.2 us (4%)
  between operations  13.5 us (4%)
  other arithmetic  3.69 us (1%)
    all_gather x1, waiting for transfers between devices, on_device(): shard_piece = lax.all_gather(slab_sums, 'pair', axis=0, tiled=True)  174 us
    all_to_all x1, waiting for transfers between devices, on_device(): lax.all_to_all(send_blocks, 'pair', split_axis=0, concat_axis=0, tiled=True)  19.8 us
    reshape x1, local copies, waits for them, and re-layouts, on_device(): shard_piece.reshape(piece_blocks * block_width, aux_count, slab_rows)  16.9 us
    all_to_all x1, blocking collectives, on_device(): lax.all_to_all(half_sums, 'occ', split_axis=3, concat_axis=2, tiled=True)  14.7 us
    all_gather x1, local copies, waits for them, and re-layouts, on_device(): shard_piece = lax.all_gather(slab_sums, 'pair', axis=0, tiled=True)  14.5 us
    dot_general x1, matrix products, on_device(): jnp.einsum('nqi,na->iqa', flat_piece, virt_coeffs, preferred_element_type...  9.58 us
    all_to_all x1, starting transfers between devices, on_device(): lax.all_to_all(send_mu, 'pair', split_axis=0, concat_axis=0, tiled=True)  7.28 us
  transfers between devices with their start and end apart: 4, of which 4 were waited for; matrix products, arithmetic and copies ran while one was open for 2% of the time, Pallas kernels for 0%

commit v1 on v0

--- a/solution.py
+++ b/solution.py
@@ -4,6 +4,12 @@
 from jax.sharding import PartitionSpec as P
 
 LIVE = 4
+
+
+def joined_along(pieces, dim):
+    pieces = jnp.moveaxis(pieces, 0, dim)
+    dims = pieces.shape
+    return pieces.reshape(*dims[:dim], dims[dim] * dims[dim + 1], *dims[dim + 2 :])
 
 
 def half_transform(block_data, mu_index, coeff_blocks):
@@ -54,7 +60,19 @@
     half_sums = summed.astype(jnp.bfloat16)
     slab_sums = lax.all_to_all(half_sums, "occ", split_axis=3, concat_axis=2, tiled=True)
     aux_count, slab_rows = (slab_sums.shape[2], slab_sums.shape[3])
-    shard_piece = lax.all_gather(slab_sums, "pair", axis=0, tiled=True)
+    size = lax.axis_size("pair")
+    pairs = [(i, (i + 1) % size) for i in range(size)]
+    back = [(b, a) for a, b in pairs]
+    lower, upper = ([], [])
+    for step in range(size - 1):
+        if step % 2 == 0:
+            lower.append(lax.ppermute(lower[-1] if lower else slab_sums, "pair", pairs))
+        else:
+            upper.append(lax.ppermute(upper[-1] if upper else slab_sums, "pair", back))
+    pieces = jnp.stack([*lower[::-1], slab_sums, *upper])
+    shift = lax.axis_index("pair") - len(lower)
+    pieces = pieces[(jnp.arange(size) - shift) % size]
+    shard_piece = joined_along(pieces, 0)
     piece_blocks = shard_piece.shape[0]
     flat_piece = shard_piece.reshape(piece_blocks * block_width, aux_count, slab_rows)
     result = jnp.einsum("nqi,na->iqa", flat_piece, virt_coeffs, preferred_element_type=jnp.float32)

time: 338 us -> 425 us (1.26)
  starting transfers between devices: 14.2 us -> 91.6 us
  local copies, waits for them, and re-layouts: 70 us -> 100 us
  between operations: 13.5 us -> 0.21 us
  waiting for transfers between devices: 204 us -> 196 us
    all_gather x1 -> x0, waiting for transfers between devices: 174 us -> none  [on_device(): shard_piece = lax.all_gather(slab_sums, 'pair', axis=0, tiled=True)]
    ppermute x0 -> x7, waiting for transfers between devices: none -> 167 us  [the longest x4 167 us: on_device(): lower.append(lax.ppermute(lower[-1] if lower else slab_sums, 'pair', pairs))]
    ppermute x0 -> x7, starting transfers between devices: none -> 77.4 us  [the longest x3 71 us: on_device(): upper.append(lax.ppermute(upper[-1] if upper else slab_sums, 'pair', back))]
    gather x0 -> x2, local copies, waits for them, and re-layouts: none -> 24.8 us  [on_device(): pieces = pieces[(jnp.arange(size) - shift) % size]]
    another operation x0 -> x2, local copies, waits for them, and re-layouts: none -> 22.8 us  [the longest x1 21.3 us: on_device(): shard_piece.reshape(piece_blocks * block_width, aux_count, slab_rows)]
    reshape x1 -> x0, local copies, waits for them, and re-layouts: 16.9 us -> none  [on_device(): shard_piece.reshape(piece_blocks * block_width, aux_count, slab_rows)]
    unnamed x7 -> x24, local copies, waits for them, and re-layouts: 4.67 us -> 20.7 us
    all_gather x1 -> x0, local copies, waits for them, and re-layouts: 14.5 us -> none  [on_device(): shard_piece = lax.all_gather(slab_sums, 'pair', axis=0, tiled=True)]
  transfers between devices with their start and end apart: 4 -> 10, of which waited for: 4 -> 7; matrix products, arithmetic and copies ran while one was open for 2% -> 5% of each run, Pallas kernels for 0% -> 0%
where the time goes in v1:
time: 425 us; the launch traced here: 424 us
  waiting for transfers between devices  196 us (46%)
  local copies, waits for them, and re-layouts  100 us (24%)
  starting transfers between devices  91.6 us (22%)
  matrix products  17.3 us (4%)
  blocking collectives  14.7 us (3%)
    ppermute x4, waiting for transfers between devices, on_device(): lower.append(lax.ppermute(lower[-1] if lower else slab_sums, 'pair', pairs))  167 us
    ppermute x3, starting transfers between devices, on_device(): upper.append(lax.ppermute(upper[-1] if upper else slab_sums, 'pair', back))  71 us
    gather x2, local copies, waits for them, and re-layouts, on_device(): pieces = pieces[(jnp.arange(size) - shift) % size]  24.8 us
    another operation x1, local copies, waits for them, and re-layouts, on_device(): shard_piece.reshape(piece_blocks * block_width, aux_count, slab_rows)  21.3 us
    unnamed x24, local copies, waits for them, and re-layouts  20.7 us
    all_to_all x1, waiting for transfers between devices, on_device(): lax.all_to_all(send_blocks, 'pair', split_axis=0, concat_axis=0, tiled=True)  19.8 us
    all_to_all x1, blocking collectives, on_device(): lax.all_to_all(half_sums, 'occ', split_axis=3, concat_axis=2, tiled=True)  14.7 us
    dot_general x1, matrix products, on_device(): jnp.einsum('nqi,na->iqa', flat_piece, virt_coeffs, preferred_element_type...  9.58 us
  transfers between devices with their start and end apart: 10, of which 7 were waited for; matrix products, arithmetic and copies ran while one was open for 5% of the time, Pallas kernels for 0%

profile of v1, /device:TPU:0, one launch (start us, length us, event | category | flops | bytes accessed | tf_op | source)
XLA Modules:
  0.0 423.7 jit_solution(5287285329561189950)
XLA Ops:
  5.3 7.3 %all-to-all-start.2 = ((s32[8,1,4]{2,1,0:T(1,128)}), s32[8,1,4]{2,1,0:T(1,128)S(1)}, u32[]{:S(2)}, u32[]{:S(2)}) async-start(s32[8,1,4]{2,1,0:T(1,128)} %bitcast.9), calls=%async_computation.2 | async-start | bytes 8192 | tf_op jit(solution)/shard_map/all_to_all | solution.py:47
  14.7 4.3 %all-to-all-done.2 = s32[8,1,4]{2,1,0:T(1,128)S(1)} async-done(((s32[8,1,4]{2,1,0:T(1,128)}), s32[8,1,4]{2,1,0:T(1,128)S(1)}, u32[]{:S(2)}, u32[]{:S(2)}) %all-to-all-start.2) | async-done | bytes 160 | tf_op jit(solution)/shard_map/all_to_all | solution.py:47
  19.0 3.3 all-to-all-start
  23.5 5.3 %all-to-all-done = s32[8,1,4]{2,1,0:T(1,128)S(1)} async-done(((s32[8,1,4]{2,1,0:T(1,128)}), s32[8,1,4]{2,1,0:T(1,128)S(1)}, u32[]{:S(2)}, u32[]{:S(2)}) %all-to-all-start) | async-done | bytes 160 | tf_op jit(solution)/shard_map/all_to_all | solution.py:48
  28.8 3.6 all-to-all-start.1
  33.3 2.8 gather_fusion.3
  36.1 19.8 %all-to-all-done.1 = bf16[8,4,64,256]{3,2,1,0:T(8,128)(2,1)S(1)} async-done(((bf16[8,4,64,256]{3,2,1,0:T(8,128)(2,1)}), bf16[8,4,64,256]{3,2,1,0:T(8,128)(2,1)S(1)}, u32[]{:S(2)}, u32[]{:S(2)}) %all-to-all-start.1) | async-done | bytes 1048608 | tf_op jit(solution)/shard_map/all_to_all | solution.py:46
  56.8 1.8 fusion.4
  58.6 5.6 %copy.46 = f32[32,64,4,128]{3,2,1,0:T(4,128)} copy(f32[32,64,4,128]{3,1,2,0:T(8,128)S(1)} %fusion.4) | data formatting | bytes 8388608 | tf_op jit(solution)/shard_map/snqm,smi->snqi/dot_general | solution.py:20
  64.2 5.7 %reshape.193 = f32[32,32768]{1,0:T(8,128)} reshape(f32[32,64,4,128]{3,2,1,0:T(4,128)} %copy.46) | data formatting | bytes 8388608 | tf_op jit(solution)/shard_map/reshape | solution.py:56
  69.8 6.1 %dot_general.15 = f32[64,4,128,32]{2,1,0,3:T(4,128)} reshape(f32[32768,32]{0,1:T(8,128)} %bitcast.69) | data formatting | bytes 8388608 | tf_op jit(solution)/shard_map/dot_general | solution.py:54
  75.9 5.9 %fusion.6 = bf16[12,64,4,128]{3,0,2,1:T(8,128)(2,1)S(1)} fusion(f32[64,4,128,32]{2,1,0,3:T(4,128)} %dot_general.15, s32[32]{0:T(128)S(1)} %and_select_fusion.1), kind=kOutput, calls=%fused_computation.19 | convolution fusion | flops 151388544 | bytes 4980864 | tf_op jit(solution)/shard_map/dot_general | solution.py:54
  81.8 4.1 copy.48
  87.4 14.7 %all_to_all.41 = bf16[4,2,49152]{2,1,0:T(2,128)(2,1)} all-to-all(bf16[4,2,49152]{2,1,0:T(2,128)(2,1)S(1)} %reshape.272), channel_id=1, replica_groups=mesh['pair'=8,'occ'=4] {'occ'}, dimensions={0} | all-to-all | bytes 1572864 | tf_op jit(solution)/shard_map/all_to_all | solution.py:61
  102.1 2.8 reshape.273
  107.0 37.2 %collective-permute-done = bf16[12,64,16,32]{1,3,2,0:T(8,128)(2,1)S(1)} collective-permute-done((bf16[12,64,16,32]{1,3,2,0:T(8,128)(2,1)S(1)}, bf16[12,64,16,32]{1,3,2,0:T(8,128)(2,1)S(1)}, u32[]{:S(2)}, u32[]{:S(2)}) %collective-permute-start) | collective-permute-done | bytes 786464 | tf_op jit(solution)/shard_map/ppermute | solution.py:69
  144.3 4.7 %collective-permute-start.4 = (bf16[12,64,16,32]{1,3,2,0:T(8,128)(2,1)S(1)}, bf16[12,64,16,32]{1,3,2,0:T(8,128)(2,1)}, u32[]{:S(2)}, u32[]{:S(2)}) collective-permute-start(bf16[12,64,16,32]{1,3,2,0:T(8,128)(2,1)S(1)} %bitcast.71), channel_id=1, source_target_pairs={{4,0},{8,4},{12,8},{16,12},{20,16},{24,20},{28,24},{0,28},{5,1},{9... | collective-permute-start | bytes 2359304 | tf_op jit(solution)/shard_map/ppermute | solution.py:71
  149.0 61.7 %collective-permute-done.1 = bf16[12,64,16,32]{1,3,2,0:T(8,128)(2,1)S(1)} collective-permute-done((bf16[12,64,16,32]{1,3,2,0:T(8,128)(2,1)S(1)}, bf16[12,64,16,32]{1,3,2,0:T(8,128)(2,1)S(1)}, u32[]{:S(2)}, u32[]{:S(2)}) %collective-permute-start.1) | collective-permute-done | bytes 786464 | tf_op jit(solution)/shard_map/ppermute | solution.py:69
  210.7 2.5 collective-permute-start.2
  213.2 32.9 %collective-permute-start.5 = (bf16[12,64,16,32]{1,3,2,0:T(8,128)(2,1)}, bf16[12,64,16,32]{1,3,2,0:T(8,128)(2,1)}, u32[]{:S(2)}, u32[]{:S(2)}) collective-permute-start(bf16[12,64,16,32]{1,3,2,0:T(8,128)(2,1)} %collective-permute-done.4), channel_id=1, source_target_pairs={{4,0},{8,4},{12,8},{16,12},{20,16},{24,20},{28,24},{0,28},{5,1},{9... | collective-permute-start | bytes 2359304 | tf_op jit(solution)/shard_map/ppermute | solution.py:71
  246.0 34.4 %collective-permute-done.2 = bf16[12,64,16,32]{1,3,2,0:T(8,128)(2,1)} collective-permute-done((bf16[12,64,16,32]{1,3,2,0:T(8,128)(2,1)S(1)}, bf16[12,64,16,32]{1,3,2,0:T(8,128)(2,1)}, u32[]{:S(2)}, u32[]{:S(2)}) %collective-permute-start.2) | collective-permute-done | bytes 786464 | tf_op jit(solution)/shard_map/ppermute | solution.py:69
  280.4 2.6 collective-permute-start.3
  283.0 33.4 %collective-permute-start.6 = (bf16[12,64,16,32]{1,3,2,0:T(8,128)(2,1)}, bf16[12,64,16,32]{1,3,2,0:T(8,128)(2,1)S(1)}, u32[]{:S(2)}, u32[]{:S(2)}) collective-permute-start(bf16[12,64,16,32]{1,3,2,0:T(8,128)(2,1)} %collective-permute-done.5), channel_id=1, source_target_pairs={{4,0},{8,4},{12,8},{16,12},{20,16},{24,20},{28,24},{0,28},{5,1},{9... | collective-permute-start | bytes 2359304 | tf_op jit(solution)/shard_map/ppermute | solution.py:71
  316.5 33.2 %collective-permute-done.3 = bf16[12,64,16,32]{1,3,2,0:T(8,128)(2,1)} collective-permute-done((bf16[12,64,16,32]{1,3,2,0:T(8,128)(2,1)}, bf16[12,64,16,32]{1,3,2,0:T(8,128)(2,1)}, u32[]{:S(2)}, u32[]{:S(2)}) %collective-permute-start.3) | collective-permute-done | bytes 786464 | tf_op jit(solution)/shard_map/ppermute | solution.py:69
  349.7 2.9 bitcast_dynamic-update-slice_fusion.6
  352.6 2.8 bitcast_dynamic-update-slice_fusion.5
  359.7 2.9 bitcast_dynamic-update-slice_fusion.2
  362.7 2.9 bitcast_dynamic-update-slice_fusion.1
  366.9 11.0 %gather_fusion.4 = bf16[8,12,64,16,32]{2,4,3,1,0:T(8,128)(2,1)} fusion(bf16[8,12,64,16,32]{2,4,3,1,0:T(8,128)(2,1)} %bitcast_dynamic-update-slice_fusion, s32[1024]{0:T(1024)S(1)} %pad_clamp_fusion), kind=kCustom, calls=%fused_computation.4 | custom fusion | bytes 12582944 | tf_op jit(solution)/shard_map/gather | solution.py:74
  377.9 13.8 %copy.52 = bf16[8,12,64,16,32]{2,1,0,4,3:T(8,128)(2,1)} copy(bf16[8,12,64,16,32]{2,4,3,1,0:T(8,128)(2,1)} %gather_fusion.4) | data formatting | bytes 12582912 | tf_op jit(solution)/shard_map/gather | solution.py:74
  391.7 21.3 %reshape_reshape.7 = bf16[6144,16,32]{0,2,1:T(8,128)(2,1)} reshape(bf16[8,12,64,16,32]{2,1,0,4,3:T(8,128)(2,1)} %copy.52) | data formatting | bytes 12582912 | tf_op jit(solution)/shard_map/reshape;reshape | solution.py:77
  413.1 9.6 %fusion.12 = bf16[32,16,640]{2,0,1:T(8,128)(2,1)S(1)} fusion(bf16[6144,16,32]{0,2,1:T(8,128)(2,1)} %reshape_reshape.7, bf16[6144,640]{1,0:T(8,128)(2,1)} %param.7), kind=kOutput, calls=%fused_computation.21 | convolution fusion | flops 4026859520 | bytes 14811136 | tf_op jit(solution)/shard_map/nqi,na->iqa/dot_general | solution.py:78
  (66 shorter events, 20.7 us)
Async XLA Ops:
  0.0 12.6 %copy-start = (bf16[1,64,64,256]{3,2,1,0:T(8,128)(2,1)S(1)}, bf16[1,64,64,256]{3,2,1,0:T(8,128)(2,1)}, u32[]{:S(2)}) copy-start(bf16[1,64,64,256]{3,2,1,0:T(8,128)(2,1)} %param.5) | copy-start | bytes 6291460
  0.0 3.9 copy-start.6
  5.3 13.7 %all-to-all-start.2 = ((s32[8,1,4]{2,1,0:T(1,128)}), s32[8,1,4]{2,1,0:T(1,128)S(1)}, u32[]{:S(2)}, u32[]{:S(2)}) async-start(s32[8,1,4]{2,1,0:T(1,128)} %bitcast.9), calls=%async_computation.2 | async-start | bytes 8192 | tf_op jit(solution)/shard_map/all_to_all | solution.py:47
  19.0 9.8 %all-to-all-start = ((s32[8,1,4]{2,1,0:T(1,128)}), s32[8,1,4]{2,1,0:T(1,128)S(1)}, u32[]{:S(2)}, u32[]{:S(2)}) async-start(s32[8,1,4]{2,1,0:T(1,128)} %bitcast.2), calls=%async_computation | async-start | bytes 8192 | tf_op jit(solution)/shard_map/all_to_all | solution.py:48
  28.8 27.1 %all-to-all-start.1 = ((bf16[8,4,64,256]{3,2,1,0:T(8,128)(2,1)}), bf16[8,4,64,256]{3,2,1,0:T(8,128)(2,1)S(1)}, u32[]{:S(2)}, u32[]{:S(2)}) async-start(bf16[8,4,64,256]{3,2,1,0:T(8,128)(2,1)} %broadcast_multiply_fusion), calls=%async_computation.1 | async-start | bytes 2097152 | tf_op jit(solution)/shard_map/all_to_all | solution.py:46
  105.7 38.5 %collective-permute-start = (bf16[12,64,16,32]{1,3,2,0:T(8,128)(2,1)S(1)}, bf16[12,64,16,32]{1,3,2,0:T(8,128)(2,1)S(1)}, u32[]{:S(2)}, u32[]{:S(2)}) collective-permute-start(bf16[12,64,16,32]{1,3,2,0:T(8,128)(2,1)S(1)} %bitcast.70), channel_id=1, source_target_pairs={{0,4},{4,8},{8,12},{12,16},{16,20},{20,24},{24,28},{28,0},{1,5},{5... | collective-permute-start | bytes 2359304 | tf_op jit(solution)/shard_map/ppermute | solution.py:69
  144.3 68.9 %copy-start.2 = (bf16[12,64,16,32]{1,3,2,0:T(8,128)(2,1)}, bf16[12,64,16,32]{1,3,2,0:T(8,128)(2,1)S(1)}, u32[]{:S(2)}) copy-start(bf16[12,64,16,32]{1,3,2,0:T(8,128)(2,1)S(1)} %collective-permute-done) | copy-start | bytes 2359300
  144.3 66.4 %collective-permute-start.1 = (bf16[12,64,16,32]{1,3,2,0:T(8,128)(2,1)S(1)}, bf16[12,64,16,32]{1,3,2,0:T(8,128)(2,1)S(1)}, u32[]{:S(2)}, u32[]{:S(2)}) collective-permute-start(bf16[12,64,16,32]{1,3,2,0:T(8,128)(2,1)S(1)} %collective-permute-done), channel_id=1, source_target_pairs={{0,4},{4,8},{8,12},{12,16},{16,20},{20,24},{24,28},{28,0},{1,5},{5... | collective-permute-start | bytes 2359304 | tf_op jit(solution)/shard_map/ppermute | solution.py:69
  144.3 68.9 %collective-permute-start.4 = (bf16[12,64,16,32]{1,3,2,0:T(8,128)(2,1)S(1)}, bf16[12,64,16,32]{1,3,2,0:T(8,128)(2,1)}, u32[]{:S(2)}, u32[]{:S(2)}) collective-permute-start(bf16[12,64,16,32]{1,3,2,0:T(8,128)(2,1)S(1)} %bitcast.71), channel_id=1, source_target_pairs={{4,0},{8,4},{12,8},{16,12},{20,16},{24,20},{28,24},{0,28},{5,1},{9... | collective-permute-start | bytes 2359304 | tf_op jit(solution)/shard_map/ppermute | solution.py:71
  210.7 35.4 %copy-start.4 = (bf16[12,64,16,32]{1,3,2,0:T(8,128)(2,1)}, bf16[12,64,16,32]{1,3,2,0:T(8,128)(2,1)S(1)}, u32[]{:S(2)}) copy-start(bf16[12,64,16,32]{1,3,2,0:T(8,128)(2,1)S(1)} %collective-permute-done.1) | copy-start | bytes 2359300
  210.7 69.7 %collective-permute-start.2 = (bf16[12,64,16,32]{1,3,2,0:T(8,128)(2,1)S(1)}, bf16[12,64,16,32]{1,3,2,0:T(8,128)(2,1)}, u32[]{:S(2)}, u32[]{:S(2)}) collective-permute-start(bf16[12,64,16,32]{1,3,2,0:T(8,128)(2,1)S(1)} %collective-permute-done.1), channel_id=1, source_target_pairs={{0,4},{4,8},{8,12},{12,16},{16,20},{20,24},{24,28},{28,0},{1,5},{5... | collective-permute-start | bytes 2359304 | tf_op jit(solution)/shard_map/ppermute | solution.py:69
  213.2 69.9 %collective-permute-start.5 = (bf16[12,64,16,32]{1,3,2,0:T(8,128)(2,1)}, bf16[12,64,16,32]{1,3,2,0:T(8,128)(2,1)}, u32[]{:S(2)}, u32[]{:S(2)}) collective-permute-start(bf16[12,64,16,32]{1,3,2,0:T(8,128)(2,1)} %collective-permute-done.4), channel_id=1, source_target_pairs={{4,0},{8,4},{12,8},{16,12},{20,16},{24,20},{28,24},{0,28},{5,1},{9... | collective-permute-start | bytes 2359304 | tf_op jit(solution)/shard_map/ppermute | solution.py:71
  280.4 69.3 %collective-permute-start.3 = (bf16[12,64,16,32]{1,3,2,0:T(8,128)(2,1)}, bf16[12,64,16,32]{1,3,2,0:T(8,128)(2,1)}, u32[]{:S(2)}, u32[]{:S(2)}) collective-permute-start(bf16[12,64,16,32]{1,3,2,0:T(8,128)(2,1)} %collective-permute-done.2), channel_id=1, source_target_pairs={{0,4},{4,8},{8,12},{12,16},{16,20},{20,24},{24,28},{28,0},{1,5},{5... | collective-permute-start | bytes 2359304 | tf_op jit(solution)/shard_map/ppermute | solution.py:69
  283.0 72.4 %copy-start.5 = (bf16[12,64,16,32]{1,3,2,0:T(8,128)(2,1)S(1)}, bf16[12,64,16,32]{1,3,2,0:T(8,128)(2,1)}, u32[]{:S(2)}) copy-start(bf16[12,64,16,32]{1,3,2,0:T(8,128)(2,1)} %copy-done.4) | copy-start | bytes 2359300
  283.0 73.8 %copy-start.3 = (bf16[12,64,16,32]{1,3,2,0:T(8,128)(2,1)S(1)}, bf16[12,64,16,32]{1,3,2,0:T(8,128)(2,1)}, u32[]{:S(2)}) copy-start(bf16[12,64,16,32]{1,3,2,0:T(8,128)(2,1)} %copy-done.2) | copy-start | bytes 2359300
  283.0 82.5 %collective-permute-start.6 = (bf16[12,64,16,32]{1,3,2,0:T(8,128)(2,1)}, bf16[12,64,16,32]{1,3,2,0:T(8,128)(2,1)S(1)}, u32[]{:S(2)}, u32[]{:S(2)}) collective-permute-start(bf16[12,64,16,32]{1,3,2,0:T(8,128)(2,1)} %collective-permute-done.5), channel_id=1, source_target_pairs={{4,0},{8,4},{12,8},{16,12},{20,16},{24,20},{28,24},{0,28},{5,1},{9... | collective-permute-start | bytes 2359304 | tf_op jit(solution)/shard_map/ppermute | solution.py:71
  413.1 10.6 %copy-start.1 = (bf16[1,64,64,256]{3,2,1,0:T(8,128)(2,1)S(1)}, bf16[1,64,64,256]{3,2,1,0:T(8,128)(2,1)}, u32[]{:S(2)}) copy-start(bf16[1,64,64,256]{3,2,1,0:T(8,128)(2,1)} %param.5) | copy-start | bytes 6291460
